TPU v7x, 32 devices: a whole 2x2x4 slice. The times are simulated.
32 devices in a mesh: tile: 16 (over z, x, core), group: 2 (over y).
Axes of the slice: x: 2, y: 2, z: 4, core: 2. Of those that a mesh axis runs over, the one named last changes fastest.
Arguments:
- object_field: float32 [2, 320, 2048], P(None, 'group', 'tile'), may hold values from -6 to 6
- probe_field: float32 [2, 256, 256], replicated, may hold values from -6 to 6
- amplitudes: float32 [32, 256, 256], P(('tile', 'group')), may hold values from 0 to 4
- row_start: int32 [32], P(('tile', 'group')), may hold values from 0 to 64
- column_start: int32 [32], P(('tile', 'group')), may hold values from 0 to 128
- live_slots: int32 [32], P(('tile', 'group')), may hold values 0 or 1
Outputs:
- new_object: float32 [2, 320, 2048], P(None, 'group', 'tile')
- new_probe: float32 [2, 256, 256], replicated
All inputs are finite; a program needn't handle non-finite values. No bound on the sum of `live_slots` on one device may be relied on, other than what follows from the above.
Results may differ from a plain program's by a relative error of at most 0.0001.
Values sent between devices are 32-bit elements; how exact they have to be, the bound alone decides.
A program may use at most 64 MiB of HBM per device.

v0:
```python
import math
import jax
import jax.numpy as jnp
from jax import lax
from jax.sharding import PartitionSpec as P

WIN = 256
HALO = 128


def padded_2(value, sides, width):
    for axis, dim in sides:
        count, length = (lax.axis_size(axis), value.shape[dim])
        up = [(i, (i + 1) % count) for i in range(count - 1)]
        down = [(j, i) for i, j in up]
        last = lax.slice_in_dim(value, length - width, length, axis=dim)
        initial = lax.slice_in_dim(value, 0, width, axis=dim)
        before = lax.ppermute(last, axis, up)
        after = lax.ppermute(initial, axis, down)
        value = jnp.concatenate([before, value, after], axis=dim)
    return value


def dft_tables(length):
    counter = jnp.arange(length, dtype=jnp.int32)
    product = counter[:, None] * counter[None, :] % length
    angles = 2.0 * math.pi / length * product.astype(jnp.float32)
    factor = 1.0 / math.sqrt(length)
    return (jnp.cos(angles) * factor, jnp.sin(angles) * factor)


def apply_left(matrix, values):
    return jnp.einsum("jk,pkl->pjl", matrix, values, precision=lax.Precision.HIGHEST)


def apply_right(values, matrix):
    return jnp.einsum("pjk,kl->pjl", values, matrix, precision=lax.Precision.HIGHEST)


def transform(real_part, imag_part, cos_table, sin_table, sign):
    left_real = apply_left(cos_table, real_part) - sign * apply_left(sin_table, imag_part)
    left_imag = apply_left(cos_table, imag_part) + sign * apply_left(sin_table, real_part)
    right_real = apply_right(left_real, cos_table) - sign * apply_right(left_imag, sin_table)
    right_imag = apply_right(left_imag, cos_table) + sign * apply_right(left_real, sin_table)
    return (right_real, right_imag)


def window_terms(windows, probe_field, amplitudes, live_slots, cos_table, sin_table):
    sample_real = windows[:, 0]
    sample_imag = windows[:, 1]
    probe_real = probe_field[0]
    probe_imag = probe_field[1]
    exit_real = probe_real * sample_real - probe_imag * sample_imag
    exit_imag = probe_real * sample_imag + probe_imag * sample_real
    far_real, far_imag = transform(exit_real, exit_imag, cos_table, sin_table, -1.0)
    modulus = jnp.maximum(jnp.sqrt(far_real * far_real + far_imag * far_imag), 0.25)
    factor = 1.0 - amplitudes / modulus
    miss_real, miss_imag = transform(
        far_real * factor, far_imag * factor, cos_table, sin_table, 1.0
    )
    weight = live_slots.astype(jnp.float32)[:, None, None]
    miss_real = miss_real * weight
    miss_imag = miss_imag * weight
    grad_real = probe_real * miss_real + probe_imag * miss_imag
    grad_imag = probe_real * miss_imag - probe_imag * miss_real
    probe_light = weight * (probe_real * probe_real + probe_imag * probe_imag)
    terms = jnp.stack([grad_real, grad_imag, probe_light], axis=1)
    probe_grad = jnp.stack(
        [
            jnp.sum(sample_real * miss_real + sample_imag * miss_imag, axis=0),
            jnp.sum(sample_real * miss_imag - sample_imag * miss_real, axis=0),
        ],
        axis=0,
    )
    window_light = jnp.sum(weight * (sample_real * sample_real + sample_imag * sample_imag), axis=0)
    return (terms, probe_grad, window_light)


def add_windows(accum, terms, top_rows, left_edges):
    zero_index = jnp.zeros((), jnp.int32)
    channels = terms.shape[1]

    def place(slot, current):
        corner = (zero_index, top_rows[slot], left_edges[slot])
        piece = lax.dynamic_slice(current, corner, (channels, WIN, WIN))
        return lax.dynamic_update_slice(current, piece + terms[slot], corner)

    return lax.fori_loop(0, terms.shape[0], place, accum)


def cut_windows(padded, top_rows, left_edges):
    zero_index = jnp.zeros((), jnp.int32)

    def single(top_row, left_edge):
        return lax.dynamic_slice(padded, (zero_index, top_row, left_edge), (2, WIN, WIN))

    return jax.vmap(single)(top_rows, left_edges)


def edge_strips(accum):
    return jnp.concatenate([accum[:, :, :HALO], accum[:, :, accum.shape[2] - HALO :]], axis=2)


def add_edges(inner, arrived):
    width = inner.shape[2]
    inner = inner.at[:, :, :HALO].add(arrived[:, :, :HALO])
    return inner.at[:, :, width - HALO :].add(arrived[:, :, arrived.shape[2] - HALO :])


def apply_updates(object_field, probe_field, share, probe_grad, window_light):
    light_max = jnp.max(probe_field[0] * probe_field[0] + probe_field[1] * probe_field[1]) + 1e-06
    new_object = object_field - share[0:2] / (share[2:3] + 0.25 * light_max)
    new_probe = (
        probe_field - probe_grad / (window_light + 0.25 * jnp.mean(window_light) + 1e-05)[None]
    )
    return (new_object, new_probe)


def local(object_field, probe_field, amplitudes, row_start, column_start, live_slots):
    cos_table, sin_table = dft_tables(WIN)
    full_rows = lax.all_gather(object_field, "group", axis=1, tiled=True)
    padded = padded_2(full_rows, (("tile", 2),), HALO)
    windows = cut_windows(padded, row_start, column_start)
    terms, probe_grad, window_light = window_terms(
        windows, probe_field, amplitudes, live_slots, cos_table, sin_table
    )
    accum = jnp.zeros((terms.shape[1], padded.shape[1], padded.shape[2]), jnp.float32)
    accum = add_windows(accum, terms, row_start, column_start)
    reduced = lax.psum_scatter(accum, "group", scatter_dimension=1, tiled=True)
    arrived = padded_2(edge_strips(reduced), (("tile", 2),), HALO)
    share = add_edges(reduced[:, :, HALO : reduced.shape[2] - HALO], arrived)
    probe_grad, window_light = lax.psum((probe_grad, window_light), ("tile", "group"))
    object_field, probe_field = apply_updates(
        object_field, probe_field, share, probe_grad, window_light
    )
    return (object_field, probe_field)


def solution(mesh):
    return jax.shard_map(
        local,
        mesh=mesh,
        in_specs=(
            P(None, "group", "tile"),
            P(),
            P(("tile", "group"), None, None),
            P(("tile", "group")),
            P(("tile", "group")),
            P(("tile", "group")),
        ),
        out_specs=(P(None, "group", "tile"), P()),
        check_vma=False,
    )
```

profile of v0, /device:TPU:3, one launch (start us, length us, event | category | flops | bytes accessed | tf_op | source)
XLA Modules:
  0.0 209.8 jit_solution(13786938275999001730)
XLA Ops:
  8.0 0.0 all-reduce.3.cloned.1.call-start
  8.1 6.1 %all_gather.3 = f32[2,320,128]{2,1,0:T(8,128)S(1)} all-gather(f32[2,160,128]{2,1,0:T(8,128)} %param.14), channel_id=1, replica_groups=mesh['tile'=16,'group'=2] {'group'}, dimensions={1}, use_global_device_ids=true | all-gather | bytes 491520 | tf_op jit(solution)/shard_map/all_gather | solution.py:121
  14.1 3.4 %collective-permute-start.1 = (f32[2,320,128]{2,1,0:T(8,128)S(1)}, f32[2,320,128]{2,1,0:T(8,128)S(1)}, u32[]{:S(2)}, u32[]{:S(2)}) collective-permute-start(f32[2,320,128]{2,1,0:T(8,128)S(1)} %all_gather.3), channel_id=1, source_target_pairs={{2,0},{4,2},{6,4},{8,6},{10,8},{12,10},{14,12},{16,14},{18,16},{20... | collective-permute-start | bytes 983048 | tf_op jit(solution)/shard_map/ppermute | solution.py:19
  17.6 3.1 %collective-permute-start = (f32[2,320,128]{2,1,0:T(8,128)S(1)}, f32[2,320,128]{2,1,0:T(8,128)S(1)}, u32[]{:S(2)}, u32[]{:S(2)}) collective-permute-start(f32[2,320,128]{2,1,0:T(8,128)S(1)} %all_gather.3), channel_id=1, source_target_pairs={{0,2},{2,4},{4,6},{6,8},{8,10},{10,12},{12,14},{14,16},{16,18},{18... | collective-permute-start | bytes 983048 | tf_op jit(solution)/shard_map/ppermute | solution.py:18
  22.6 1.0 collective-permute-done.1
  23.6 1.1 collective-permute-done
  24.7 0.4 fusion.12
  25.1 0.1 fusion.39
  25.2 1.5 fusion.37
  26.7 1.5 fusion.33
  28.2 1.5 fusion.9
  29.6 1.5 fusion.7
  31.1 1.5 fusion.48
  32.6 0.0 copy-start.4
  32.6 1.5 fusion.49
  34.1 1.5 fusion.4
  35.6 1.7 bitcast_multiply_fusion.11
  37.4 1.5 fusion.30
  38.8 1.5 fusion.26
  40.3 1.5 fusion.3
  41.8 1.5 fusion.2
  43.3 1.5 fusion.46
  44.8 1.5 fusion.47
  46.3 1.5 fusion
  47.8 1.7 fusion.1
  49.5 0.8 fusion.17
  50.3 0.8 pad_maximum_fusion
  51.1 0.0 all-reduce.3.cloned.1.call-update
  51.1 0.0 reduce-scatter.2.cloned.1.call-start
  51.2 0.7 fusion.23
  51.9 0.1 maximum_bitcast_fusion
  51.9 0.1 broadcast_in_dim.6
  52.0 9.9 %dynamic_update_slice.4 = f32[3,320,384]{2,1,0:T(8,128)S(1)} dynamic-update-slice(f32[3,320,384]{2,1,0:T(8,128)S(1)} %broadcast_in_dim.6, f32[3,256,256]{2,1,0:T(8,128)S(1)} %maximum_bitcast_fusion, s32[]{:T(128)} %constant.112.clone.1, s32[]{:T(128)S(6)} %select_n.60, s32[]{:T(128)S(6)} %select_n.61) | dynamic-update-slice | bytes 1572868 | tf_op jit(solution)/shard_map/while/body/eval_jaxpr/dynamic_update_slice | solution.py:86
  61.9 1.1 copy-done
  63.0 0.0 reduce-scatter.2.cloned.1.call-update
  63.7 119.6 %all-reduce.3.cloned.1.call-done = (f32[2,256,256]{2,1,0:T(8,128)}, f32[256,256]{1,0:T(8,128)}) async-done(((f32[2,256,256]{2,1,0:T(8,128)}, f32[256,256]{1,0:T(8,128)}), (f32[2,256,256]{2,1,0:T(8,128)}, f32[256,256]{1,0:T(8,128)})) %all-reduce.3.cloned.1.call-update) | async-done | bytes 786448 | tf_op jit(solution)/shard_map/psum | solution.py:132
  183.3 1.7 reduce_sum.8
  185.6 1.0 add_add_fusion
  186.6 0.0 reduce-scatter.2.cloned.1.call-done
  186.6 1.1 fusion.132
  187.7 4.5 %collective-permute-start.2 = (f32[3,160,128]{2,1,0:T(8,128)S(1)}, f32[3,160,128]{2,1,0:T(8,128)S(1)}, u32[]{:S(2)}, u32[]{:S(2)}) collective-permute-start(f32[3,160,128]{2,1,0:T(8,128)S(1)} %get-tuple-element.81), channel_id=1, source_target_pairs={{0,2},{2,4},{4,6},{6,8},{8,10},{10,12},{12,14},{14,16},{16,18},{18... | collective-permute-start | bytes 737288 | tf_op jit(solution)/shard_map/ppermute | solution.py:18
  192.2 1.9 collective-permute-start.3
  194.1 0.0 copy-start.2
  194.2 0.9 divide_subtract_fusion
  195.0 0.3 collective-permute-done.2
  195.3 5.3 %collective-permute-done.3 = f32[3,160,128]{2,1,0:T(8,128)S(1)} collective-permute-done((f32[3,160,128]{2,1,0:T(8,128)S(1)}, f32[3,160,128]{2,1,0:T(8,128)S(1)}, u32[]{:S(2)}, u32[]{:S(2)}) %collective-permute-start.3) | collective-permute-done | bytes 245792 | tf_op jit(solution)/shard_map/ppermute | solution.py:19
  200.6 1.0 fusion.44
  201.6 0.7 fusion.45
  (8 shorter events, 0.0 us)
Async XLA Ops:
  8.0 17.1 %copy-start.1 = (f32[2,256,256]{2,1,0:T(8,128)S(1)}, f32[2,256,256]{2,1,0:T(8,128)}, u32[]{:S(2)}) copy-start(f32[2,256,256]{2,1,0:T(8,128)} %param.15) | copy-start | bytes 1572868
  8.0 175.3 %all-reduce.3.cloned.1.call-start = ((), (), s32[]{:S(2)}) async-start(), calls=%async_computation.2 | async-start | bytes 1572864 | tf_op jit(solution)/shard_map/psum | solution.py:132
  14.1 9.4 %collective-permute-start.1 = (f32[2,320,128]{2,1,0:T(8,128)S(1)}, f32[2,320,128]{2,1,0:T(8,128)S(1)}, u32[]{:S(2)}, u32[]{:S(2)}) collective-permute-start(f32[2,320,128]{2,1,0:T(8,128)S(1)} %all_gather.3), channel_id=1, source_target_pairs={{2,0},{4,2},{6,4},{8,6},{10,8},{12,10},{14,12},{16,14},{18,16},{20... | collective-permute-start | bytes 983048 | tf_op jit(solution)/shard_map/ppermute | solution.py:19
  17.6 7.1 %collective-permute-start = (f32[2,320,128]{2,1,0:T(8,128)S(1)}, f32[2,320,128]{2,1,0:T(8,128)S(1)}, u32[]{:S(2)}, u32[]{:S(2)}) collective-permute-start(f32[2,320,128]{2,1,0:T(8,128)S(1)} %all_gather.3), channel_id=1, source_target_pairs={{0,2},{2,4},{4,6},{6,8},{8,10},{10,12},{12,14},{14,16},{16,18},{18... | collective-permute-start | bytes 983048 | tf_op jit(solution)/shard_map/ppermute | solution.py:18
  32.6 3.0 %copy-start.4 = (f32[1,256,256]{2,1,0:T(8,128)S(1)}, f32[1,256,256]{2,1,0:T(8,128)}, u32[]{:S(2)}) copy-start(f32[1,256,256]{2,1,0:T(8,128)} %param.16) | copy-start | bytes 786436
  51.1 135.5 %reduce-scatter.2.cloned.1.call-start = ((), (), s32[]{:S(2)}) async-start(), calls=%async_computation.1 | async-start | bytes 2211840 | tf_op jit(solution)/shard_map/reduce_scatter | solution.py:129
  61.9 1.1 copy-start
  183.3 10.9 %copy-start.3 = (f32[2,256,256]{2,1,0:T(8,128)S(1)}, f32[2,256,256]{2,1,0:T(8,128)}, u32[]{:S(2)}) copy-start(f32[2,256,256]{2,1,0:T(8,128)} %get-tuple-element.71) | copy-start | bytes 1572868
  187.7 7.6 %collective-permute-start.2 = (f32[3,160,128]{2,1,0:T(8,128)S(1)}, f32[3,160,128]{2,1,0:T(8,128)S(1)}, u32[]{:S(2)}, u32[]{:S(2)}) collective-permute-start(f32[3,160,128]{2,1,0:T(8,128)S(1)} %get-tuple-element.81), channel_id=1, source_target_pairs={{0,2},{2,4},{4,6},{6,8},{8,10},{10,12},{12,14},{14,16},{16,18},{18... | collective-permute-start | bytes 737288 | tf_op jit(solution)/shard_map/ppermute | solution.py:18
  192.2 8.4 %collective-permute-start.3 = (f32[3,160,128]{2,1,0:T(8,128)S(1)}, f32[3,160,128]{2,1,0:T(8,128)S(1)}, u32[]{:S(2)}, u32[]{:S(2)}) collective-permute-start(f32[3,160,128]{2,1,0:T(8,128)S(1)} %get-tuple-element.82), channel_id=1, source_target_pairs={{2,0},{4,2},{6,4},{8,6},{10,8},{12,10},{14,12},{16,14},{18,16},{20... | collective-permute-start | bytes 737288 | tf_op jit(solution)/shard_map/ppermute | solution.py:19
  194.1 7.5 %copy-start.2 = (f32[2,160,128]{2,1,0:T(8,128)S(1)}, f32[2,160,128]{2,1,0:T(8,128)}, u32[]{:S(2)}) copy-start(f32[2,160,128]{2,1,0:T(8,128)} %param.14) | copy-start | bytes 491524
Sparse Core Ops, SparseCore 0:
  51.2 131.9 all-reduce.2
Sparse Core Ops, SparseCore 1:
  63.1 27.8 reduce-scatter.1
where the time goes:
time: 210 us
  waiting for transfers between devices  127 us (60%)
  matrix products  24.1 us (11%)
  between operations  19 us (9%)
  starting transfers between devices  13 us (6%)
  local copies, waits for them, and re-layouts  12.2 us (6%)
  other arithmetic  8.07 us (4%)
  blocking collectives  6.09 us (3%)
    psum x1, waiting for transfers between devices, local(): lax.psum((probe_grad, window_light), ('tile', 'group'))  120 us
    dot_general x8, matrix products, apply_right(): jnp.einsum('pjk,kl->pjl', values, matrix, precision=lax.Precision.HIGHEST)  12.3 us
    dot_general x8, matrix products, apply_left(): jnp.einsum('jk,pkl->pjl', matrix, values, precision=lax.Precision.HIGHEST)  11.8 us
    dynamic_update_slice x1, local copies, waits for them, and re-layouts, place(): return lax.dynamic_update_slice(current, piece + terms[slot], corner)  9.85 us
    ppermute x2, starting transfers between devices, padded_2(): before = lax.ppermute(last, axis, up)  7.55 us
    ppermute x2, waiting for transfers between devices, padded_2(): after = lax.ppermute(initial, axis, down)  6.25 us
    all_gather x1, blocking collectives, local(): full_rows = lax.all_gather(object_field, 'group', axis=1, tiled=True)  6.09 us
    ppermute x2, starting transfers between devices, padded_2(): after = lax.ppermute(initial, axis, down)  5.35 us
  transfers between devices with their start and end apart: 6, of which 5 were waited for; matrix products, arithmetic and copies ran while one was open for 7% of the time, Pallas kernels for 0%

commit v1 on v0

--- a/solution.py
+++ b/solution.py
@@ -129,7 +129,13 @@
     reduced = lax.psum_scatter(accum, "group", scatter_dimension=1, tiled=True)
     arrived = padded_2(edge_strips(reduced), (("tile", 2),), HALO)
     share = add_edges(reduced[:, :, HALO : reduced.shape[2] - HALO], arrived)
-    probe_grad, window_light = lax.psum((probe_grad, window_light), ("tile", "group"))
+
+    def show_tasks_all(xx):
+        for m in ("group", "tile"):
+            xx = lax.psum(xx, m)
+        return xx
+
+    probe_grad, window_light = show_tasks_all((probe_grad, window_light))
     object_field, probe_field = apply_updates(
         object_field, probe_field, share, probe_grad, window_light
     )

time: 210 us -> 232 us (1.10)
  waiting for transfers between devices: 127 us -> 151 us
    reduce_scatter x1, waiting for transfers between devices: 0.03 us -> 24.7 us  [local(): reduced = lax.psum_scatter(accum, 'group', scatter_dimension=1, tiled=True)]
    psum x1 -> x2, waiting for transfers between devices: 120 us -> 119 us  [show_tasks_all(): xx = lax.psum(xx, m)]
  transfers between devices with their start and end apart: 6 -> 7, of which waited for: 5 -> 7; matrix products, arithmetic and copies ran while one was open for 7% -> 6% of each run, Pallas kernels for 0% -> 0%
where the time goes in v1:
time: 232 us
  waiting for transfers between devices  151 us (65%)
  matrix products  24.1 us (10%)
  between operations  17.3 us (7%)
  starting transfers between devices  12.4 us (5%)
  local copies, waits for them, and re-layouts  12.2 us (5%)
  other arithmetic  8.11 us (3%)
  blocking collectives  6.09 us (3%)
    psum x2, waiting for transfers between devices, show_tasks_all(): xx = lax.psum(xx, m)  119 us
    reduce_scatter x1, waiting for transfers between devices, local(): reduced = lax.psum_scatter(accum, 'group', scatter_dimension=1, tiled=True)  24.7 us
    dot_general x8, matrix products, apply_right(): jnp.einsum('pjk,kl->pjl', values, matrix, precision=lax.Precision.HIGHEST)  12.3 us
    dot_general x8, matrix products, apply_left(): jnp.einsum('jk,pkl->pjl', matrix, values, precision=lax.Precision.HIGHEST)  11.8 us
    dynamic_update_slice x1, local copies, waits for them, and re-layouts, place(): return lax.dynamic_update_slice(current, piece + terms[slot], corner)  9.85 us
    ppermute x2, starting transfers between devices, padded_2(): before = lax.ppermute(last, axis, up)  6.92 us
    ppermute x2, waiting for transfers between devices, padded_2(): after = lax.ppermute(initial, axis, down)  6.26 us
    all_gather x1, blocking collectives, local(): full_rows = lax.all_gather(object_field, 'group', axis=1, tiled=True)  6.09 us
  transfers between devices with their start and end apart: 7, of which 7 were waited for; matrix products, arithmetic and copies ran while one was open for 6% of the time, Pallas kernels for 0%

profile of v1, /device:TPU:3, one launch (start us, length us, event | category | flops | bytes accessed | tf_op | source)
XLA Modules:
  0.0 231.6 jit_solution(10477526555658630507)
XLA Ops:
  7.2 0.0 all-reduce.7.cloned.1.call-start
  7.2 6.1 %all_gather.3 = f32[2,320,128]{2,1,0:T(8,128)S(1)} all-gather(f32[2,160,128]{2,1,0:T(8,128)} %param.14), channel_id=1, replica_groups=mesh['tile'=16,'group'=2] {'group'}, dimensions={1}, use_global_device_ids=true | all-gather | bytes 491520 | tf_op jit(solution)/shard_map/all_gather | solution.py:121
  13.3 3.4 %collective-permute-start.1 = (f32[2,320,128]{2,1,0:T(8,128)S(1)}, f32[2,320,128]{2,1,0:T(8,128)S(1)}, u32[]{:S(2)}, u32[]{:S(2)}) collective-permute-start(f32[2,320,128]{2,1,0:T(8,128)S(1)} %all_gather.3), channel_id=1, source_target_pairs={{2,0},{4,2},{6,4},{8,6},{10,8},{12,10},{14,12},{16,14},{18,16},{20... | collective-permute-start | bytes 983048 | tf_op jit(solution)/shard_map/ppermute | solution.py:19
  16.7 3.1 %collective-permute-start = (f32[2,320,128]{2,1,0:T(8,128)S(1)}, f32[2,320,128]{2,1,0:T(8,128)S(1)}, u32[]{:S(2)}, u32[]{:S(2)}) collective-permute-start(f32[2,320,128]{2,1,0:T(8,128)S(1)} %all_gather.3), channel_id=1, source_target_pairs={{0,2},{2,4},{4,6},{6,8},{8,10},{10,12},{12,14},{14,16},{16,18},{18... | collective-permute-start | bytes 983048 | tf_op jit(solution)/shard_map/ppermute | solution.py:18
  21.8 1.0 collective-permute-done.1
  22.7 1.1 collective-permute-done
  23.9 0.4 fusion.12
  24.3 0.1 fusion.39
  24.4 1.5 fusion.37
  25.9 1.5 fusion.33
  27.3 1.5 fusion.9
  28.8 1.5 fusion.7
  30.3 1.5 fusion.48
  31.8 1.5 fusion.49
  33.3 1.5 fusion.4
  34.8 1.7 bitcast_multiply_fusion.11
  36.5 1.5 fusion.30
  38.0 1.5 fusion.26
  39.5 1.5 fusion.3
  41.0 1.5 fusion.2
  42.5 1.5 fusion.46
  44.0 1.5 fusion.47
  45.4 1.5 fusion
  46.9 1.7 fusion.1
  48.6 0.8 fusion.17
  49.5 0.8 pad_maximum_fusion
  50.3 0.0 all-reduce.7.cloned.1.call-update
  50.3 0.0 all-reduce.5.cloned.1.call-start
  50.4 36.8 %all-reduce.7.cloned.1.call-done = (f32[2,256,256]{2,1,0:T(8,128)}, f32[256,256]{1,0:T(8,128)}) async-done(((f32[2,256,256]{2,1,0:T(8,128)}, f32[256,256]{1,0:T(8,128)}), (f32[2,256,256]{2,1,0:T(8,128)}, f32[256,256]{1,0:T(8,128)})) %all-reduce.7.cloned.1.call-update) | async-done | bytes 786448 | tf_op jit(solution)/shard_map/psum | solution.py:135
  87.2 0.0 all-reduce.5.cloned.1.call-update
  87.2 0.0 reduce-scatter.2.cloned.1.call-start
  87.3 0.7 fusion.23
  88.0 0.1 maximum_bitcast_fusion
  88.0 0.1 broadcast_in_dim.6
  88.1 9.9 %dynamic_update_slice.4 = f32[3,320,384]{2,1,0:T(8,128)S(1)} dynamic-update-slice(f32[3,320,384]{2,1,0:T(8,128)S(1)} %broadcast_in_dim.6, f32[3,256,256]{2,1,0:T(8,128)S(1)} %maximum_bitcast_fusion, s32[]{:T(128)} %constant.112.clone.1, s32[]{:T(128)S(6)} %select_n.60, s32[]{:T(128)S(6)} %select_n.61) | dynamic-update-slice | bytes 1572868 | tf_op jit(solution)/shard_map/while/body/eval_jaxpr/dynamic_update_slice | solution.py:86
  98.0 1.1 copy-done
  99.8 82.2 %all-reduce.5.cloned.1.call-done = (f32[2,256,256]{2,1,0:T(8,128)}, f32[256,256]{1,0:T(8,128)}) async-done(((f32[2,256,256]{2,1,0:T(8,128)}, f32[256,256]{1,0:T(8,128)}), (f32[2,256,256]{2,1,0:T(8,128)}, f32[256,256]{1,0:T(8,128)})) %all-reduce.5.cloned.1.call-update) | async-done | bytes 786448 | tf_op jit(solution)/shard_map/psum | solution.py:135
  182.0 1.7 reduce_sum.8
  184.4 1.0 add_add_fusion
  185.4 24.7 %reduce-scatter.2.cloned.1.call-done = f32[3,160,384]{2,1,0:T(8,128)} async-done(((f32[3,320,384]{2,1,0:T(8,128)}), f32[3,160,384]{2,1,0:T(8,128)}) %reduce-scatter.2.cloned.1.call-update) | async-done | bytes 737296 | tf_op jit(solution)/shard_map/reduce_scatter | solution.py:129
  210.0 1.1 fusion.132
  211.1 3.8 %collective-permute-start.2 = (f32[3,160,128]{2,1,0:T(8,128)S(1)}, f32[3,160,128]{2,1,0:T(8,128)S(1)}, u32[]{:S(2)}, u32[]{:S(2)}) collective-permute-start(f32[3,160,128]{2,1,0:T(8,128)S(1)} %get-tuple-element.83), channel_id=1, source_target_pairs={{0,2},{2,4},{4,6},{6,8},{8,10},{10,12},{12,14},{14,16},{16,18},{18... | collective-permute-start | bytes 737288 | tf_op jit(solution)/shard_map/ppermute | solution.py:18
  215.0 1.9 collective-permute-start.3
  216.9 0.9 divide_subtract_fusion
  217.8 0.3 collective-permute-done.2
  218.1 5.3 %collective-permute-done.3 = f32[3,160,128]{2,1,0:T(8,128)S(1)} collective-permute-done((f32[3,160,128]{2,1,0:T(8,128)S(1)}, f32[3,160,128]{2,1,0:T(8,128)S(1)}, u32[]{:S(2)}, u32[]{:S(2)}) %collective-permute-start.3) | collective-permute-done | bytes 245792 | tf_op jit(solution)/shard_map/ppermute | solution.py:19
  223.4 1.0 fusion.44
  224.4 0.7 fusion.45
  (11 shorter events, 0.0 us)
Async XLA Ops:
  7.2 17.1 %copy-start.1 = (f32[2,256,256]{2,1,0:T(8,128)S(1)}, f32[2,256,256]{2,1,0:T(8,128)}, u32[]{:S(2)}) copy-start(f32[2,256,256]{2,1,0:T(8,128)} %param.15) | copy-start | bytes 1572868
  7.2 80.0 %all-reduce.7.cloned.1.call-start = ((), (), s32[]{:S(2)}) async-start(), calls=%async_computation.3 | async-start | bytes 1572864 | tf_op jit(solution)/shard_map/psum | solution.py:135
  13.3 9.4 %collective-permute-start.1 = (f32[2,320,128]{2,1,0:T(8,128)S(1)}, f32[2,320,128]{2,1,0:T(8,128)S(1)}, u32[]{:S(2)}, u32[]{:S(2)}) collective-permute-start(f32[2,320,128]{2,1,0:T(8,128)S(1)} %all_gather.3), channel_id=1, source_target_pairs={{2,0},{4,2},{6,4},{8,6},{10,8},{12,10},{14,12},{16,14},{18,16},{20... | collective-permute-start | bytes 983048 | tf_op jit(solution)/shard_map/ppermute | solution.py:19
  16.7 7.1 %collective-permute-start = (f32[2,320,128]{2,1,0:T(8,128)S(1)}, f32[2,320,128]{2,1,0:T(8,128)S(1)}, u32[]{:S(2)}, u32[]{:S(2)}) collective-permute-start(f32[2,320,128]{2,1,0:T(8,128)S(1)} %all_gather.3), channel_id=1, source_target_pairs={{0,2},{2,4},{4,6},{6,8},{8,10},{10,12},{12,14},{14,16},{16,18},{18... | collective-permute-start | bytes 983048 | tf_op jit(solution)/shard_map/ppermute | solution.py:18
  31.8 3.0 %copy-start.4 = (f32[1,256,256]{2,1,0:T(8,128)S(1)}, f32[1,256,256]{2,1,0:T(8,128)}, u32[]{:S(2)}) copy-start(f32[1,256,256]{2,1,0:T(8,128)} %param.16) | copy-start | bytes 786436
  50.3 131.7 %all-reduce.5.cloned.1.call-start = ((), (), s32[]{:S(2)}) async-start(), calls=%async_computation.2 | async-start | bytes 1572864 | tf_op jit(solution)/shard_map/psum | solution.py:135
  87.2 122.8 %reduce-scatter.2.cloned.1.call-start = ((), (), s32[]{:S(2)}) async-start(), calls=%async_computation.1 | async-start | bytes 2211840 | tf_op jit(solution)/shard_map/reduce_scatter | solution.py:129
  98.0 1.1 copy-start
  182.0 34.9 %copy-start.3 = (f32[2,256,256]{2,1,0:T(8,128)S(1)}, f32[2,256,256]{2,1,0:T(8,128)}, u32[]{:S(2)}) copy-start(f32[2,256,256]{2,1,0:T(8,128)} %get-tuple-element.71) | copy-start | bytes 1572868
  211.1 7.0 %collective-permute-start.2 = (f32[3,160,128]{2,1,0:T(8,128)S(1)}, f32[3,160,128]{2,1,0:T(8,128)S(1)}, u32[]{:S(2)}, u32[]{:S(2)}) collective-permute-start(f32[3,160,128]{2,1,0:T(8,128)S(1)} %get-tuple-element.83), channel_id=1, source_target_pairs={{0,2},{2,4},{4,6},{6,8},{8,10},{10,12},{12,14},{14,16},{16,18},{18... | collective-permute-start | bytes 737288 | tf_op jit(solution)/shard_map/ppermute | solution.py:18
  215.0 8.4 %collective-permute-start.3 = (f32[3,160,128]{2,1,0:T(8,128)S(1)}, f32[3,160,128]{2,1,0:T(8,128)S(1)}, u32[]{:S(2)}, u32[]{:S(2)}) collective-permute-start(f32[3,160,128]{2,1,0:T(8,128)S(1)} %get-tuple-element.84), channel_id=1, source_target_pairs={{2,0},{4,2},{6,4},{8,6},{10,8},{12,10},{14,12},{16,14},{18,16},{20... | collective-permute-start | bytes 737288 | tf_op jit(solution)/shard_map/ppermute | solution.py:19
  216.9 7.5 %copy-start.2 = (f32[2,160,128]{2,1,0:T(8,128)S(1)}, f32[2,160,128]{2,1,0:T(8,128)}, u32[]{:S(2)}) copy-start(f32[2,160,128]{2,1,0:T(8,128)} %param.14) | copy-start | bytes 491524
Sparse Core Ops, SparseCore 0:
  50.4 36.7 all-reduce.6
  90.7 91.2 all-reduce.4
  184.3 25.6 reduce-scatter.1
